TPU v7x, 256 devices: a whole 4x4x8 slice. The times are simulated.
256 devices in a mesh: grp: 2 (over core), fsdp: 16 (over y, z_lo), tp: 8 (over x, z_hi).
Axes of the slice: x: 4, y: 4, z: 8 (z_hi: 2, z_lo: 4; z = z_hi * 4 + z_lo), core: 2. Of those that a mesh axis runs over, the one named last changes fastest.
Arguments:
- frames: bfloat16 [2, 4096, 8192], P('grp', 'fsdp'), may hold values from -6 to 6
- rewards: bfloat16 [4096], P('fsdp'), may hold values from -5 to 5
- actions: int32 [2, 4096], P('grp', 'fsdp'), may hold values from 0 to 17
- fractions: int32 [2, 4096, 32], P('grp', 'fsdp'), may hold values from 0 to 63
- episode_shard: int32 [4096, 1], P('fsdp'), may hold values from 0 to 15, as said below
- table: float32 [64], replicated, may hold values from 0.02 to 0.98
- norm_gain: float32 [8192], replicated, may hold values from 0.1 to 1.9
- torso_weight: bfloat16 [8192, 4096], P(('grp', 'fsdp'), 'tp'), may hold values from -0.0625 to 0.0625
- embed_weight: bfloat16 [64, 4096], P(None, 'tp'), may hold values from -0.75 to 0.75
- value_weight: bfloat16 [18, 4096], P(None, 'tp'), may hold values from -0.59765625 to 0.59765625
Outputs:
- torso_grad: float32 [8192, 4096], P(('grp', 'fsdp'), 'tp')
- refreshed_weight: bfloat16 [8192, 4096], P(('grp', 'fsdp', 'tp'))
Inputs may be any that keep to these rules, and one draw needn't show every extreme that they name: `episode_shard`: of the rows of one index of fsdp, at most 24 belong to one learner shard, and in every such block some learner shard gets exactly 24; every learner shard gets at least one row from every block.
All inputs are finite; a program needn't handle non-finite values.
Results may differ from a plain program's by a relative error of at most 0.0075.
Values may be sent and summed in bfloat16 or wider, within the bound.
No kernel may reach another device: no remote copies, remote signals or barrier semaphores. Data moves between devices by JAX's collectives and lax.ppermute only.
A program may use at most 64 MiB of HBM per device.

v0:
```python
import jax
import jax.numpy as jnp
from jax import lax
from jax.sharding import PartitionSpec as P

ACTIONS = 18
COSINES = 64
FRACS = 64


def shards(
    frames,
    rewards,
    actions,
    fractions,
    episode_shard,
    table,
    norm_gain,
    torso_weight,
    embed_weight,
    value_weight,
):
    shard_total = lax.axis_size("fsdp")
    destination = episode_shard[:, 0]
    rows_block = destination.shape[0]
    lanes = jnp.arange(shard_total, dtype=jnp.int32)
    onehot = (destination[:, None] == lanes[None, :]).astype(jnp.int32)
    counts = lax.psum(jnp.sum(onehot.astype(jnp.float32), axis=0), "fsdp")
    row_weight = jnp.dot(
        onehot.astype(jnp.float32), float(rows_block) / counts, precision=lax.Precision.HIGHEST
    )
    rows_data = frames[0]
    action_rows = actions[0]
    fraction_rows = fractions[0]
    values = rows_data.astype(jnp.float32)
    mean_square = jnp.mean(values * values, axis=-1, keepdims=True)
    normed = (values * lax.rsqrt(mean_square + 1e-05) * norm_gain).astype(jnp.bfloat16)
    columns = normed
    preact = jnp.dot(
        columns,
        lax.all_gather(torso_weight, ("grp", "fsdp"), axis=0, tiled=True),
        preferred_element_type=jnp.float32,
    )
    choose_mask = (action_rows[:, None] == jnp.arange(ACTIONS, dtype=jnp.int32)[None, :]).astype(
        jnp.bfloat16
    )
    picked = jnp.dot(choose_mask, value_weight, preferred_element_type=jnp.float32)
    weighted = (jax.nn.silu(preact) * picked).astype(jnp.bfloat16)
    cosine = jnp.cos(
        jnp.pi * jnp.arange(COSINES, dtype=jnp.float32)[None, :] * table[:, None]
    ).astype(jnp.bfloat16)
    embedding = jax.nn.relu(
        jnp.dot(cosine, embed_weight, preferred_element_type=jnp.float32)
    ).astype(jnp.bfloat16)
    table_values = lax.dot_general(
        weighted, embedding, (((1,), (1,)), ((), ())), preferred_element_type=jnp.float32
    )
    selector = (
        fraction_rows[:, :, None] == jnp.arange(FRACS, dtype=jnp.int32)[None, None, :]
    ).astype(jnp.float32)
    partial_quant = jnp.einsum(
        "mj,mtj->mt", table_values, selector, precision=lax.Precision.HIGHEST
    )
    group_index = lax.axis_index("grp")
    own_slot = jnp.arange(2, dtype=jnp.int32)[:, None, None] == group_index
    stacked = jnp.where(
        own_slot, partial_quant[None, :, :], jnp.zeros_like(partial_quant)[None, :, :]
    )
    summed = lax.psum(stacked, ("grp", "tp"))
    target_quant = summed[0]
    online_quant = summed[1]
    learner = (group_index == 1).astype(jnp.float32)
    levels = jnp.einsum("mtj,j->mt", selector, table, precision=lax.Precision.HIGHEST)
    target_value = rewards.astype(jnp.float32)[:, None] + 0.99 * target_quant
    errors = target_value[:, None, :] - online_quant[:, :, None]
    weight = jnp.abs(levels[:, :, None] - (errors < 0).astype(jnp.float32))
    grad_quant = -(learner * row_weight)[:, None] * jnp.sum(
        weight * jnp.clip(errors, -1.0, 1.0), axis=-1
    )
    grad_table = jnp.einsum("mi,mij->mj", grad_quant, selector, precision=lax.Precision.HIGHEST)
    grad_feature = jnp.dot(
        grad_table, embedding.astype(jnp.float32), precision=lax.Precision.HIGHEST
    )
    gate_value = jax.nn.sigmoid(preact)
    grad_preact = (grad_feature * picked * gate_value * (1.0 + preact * (1.0 - gate_value))).astype(
        jnp.bfloat16
    )
    columns = normed
    torso_grad = lax.psum_scatter(
        lax.dot_general(
            columns, grad_preact, (((0,), (0,)), ((), ())), preferred_element_type=jnp.float32
        ),
        ("grp", "fsdp"),
        scatter_dimension=0,
        tiled=True,
    )
    updated = (torso_weight.astype(jnp.float32) - 0.01 * torso_grad).astype(jnp.bfloat16)
    refreshed_weight = lax.all_to_all(updated, "tp", split_axis=0, concat_axis=1, tiled=True)
    return (torso_grad, refreshed_weight)


def solution(mesh):
    placed = (
        P("grp", "fsdp", None),
        P("fsdp"),
        P("grp", "fsdp"),
        P("grp", "fsdp", None),
        P("fsdp", None),
        P(),
        P(),
        P(("grp", "fsdp"), "tp"),
        P(None, "tp"),
        P(None, "tp"),
    )
    return jax.shard_map(
        shards,
        mesh=mesh,
        in_specs=placed,
        out_specs=(P(("grp", "fsdp"), "tp"), P(("grp", "fsdp", "tp"), None)),
        check_vma=False,
    )
```

profile of v0, /device:TPU:1, one launch (start us, length us, event | category | flops | bytes accessed | tf_op | source)
XLA Modules:
  0.0 676.3 jit_solution(3532035005112224799)
XLA Ops:
  7.3 0.7 all-gather.2.cloned.1.call-update
  8.0 0.8 convert_reduce_fusion
  8.8 39.0 %psum.14 = f32[16]{0:T(128)S(1)} all-reduce(f32[16]{0:T(128)S(1)} %convert_reduce_fusion), channel_id=1, replica_groups=mesh['grp'=2,'fsdp'=16,'tp'=8] {'fsdp'}, use_global_device_ids=true, to_apply=%region_2.0 | all-reduce | flops 16 | bytes 128 | tf_op jit(solution)/shard_map/psum | solution.py:28
  47.8 3.2 fusion
  51.1 0.3 fusion.12
  51.5 0.3 fusion.19
  51.7 3.8 fusion.15
  55.5 27.9 %all-gather.2.cloned.1.call-done = bf16[8192,512]{1,0:T(8,128)(2,1)} async-done(((bf16[256,512]{1,0:T(8,128)(2,1)}), bf16[8192,512]{1,0:T(8,128)(2,1)}) %all-gather.2.cloned.1.call-update) | async-done | bytes 8388624 | tf_op jit(solution)/shard_map/all_gather | solution.py:41
  83.4 7.0 %fusion.10 = f32[256,512]{1,0:T(8,128)S(1)} fusion(bf16[8192,512]{1,0:T(8,128)(2,1)} %all-gather.2.cloned.1.call-done, bf16[1,256,8192]{2,1,0:T(8,128)(2,1)} %param.10, f32[8192]{0:T(1024)S(1)} %copy-done.3, f32[256]{0:T(256)S(1)} %add_rsqrt_fusion), kind=kOutput, calls=%fused_computation.17 | convolution fusion | flops 2155872256 | bytes 13140992 | tf_op jit(solution)/shard_map/dot_general | solution.py:39
  90.5 0.3 fusion.18
  90.8 0.4 select_reduce_fusion.1
  91.1 0.7 broadcast_select_fusion
  91.9 2.8 copy.17
  94.8 172.4 %all-reduce.2.cloned.1.call-done = f32[2,256,32]{1,2,0:T(8,128)} async-done(((f32[2,256,32]{1,2,0:T(8,128)}), f32[2,256,32]{1,2,0:T(8,128)}) %all-reduce.2.cloned.1.call-update) | async-done | bytes 65552 | tf_op jit(solution)/shard_map/psum | solution.py:69
  267.1 0.8 slice_bitcast_fusion
  267.9 0.8 fusion.22
  268.7 0.3 fusion.14
  269.0 0.4 select_reduce_fusion
  269.4 0.5 fusion.7
  270.0 10.4 %fusion.8 = f32[8192,512]{1,0:T(8,128)} fusion(bf16[256,512]{1,0:T(8,128)(2,1)S(1)} %fusion.7, bf16[1,256,8192]{2,1,0:T(8,128)(2,1)} %param.10, f32[8192]{0:T(1024)S(1)} %copy-done.3, f32[256]{0:T(256)S(1)} %add_rsqrt_fusion), kind=kOutput, calls=%fused_computation.16 | convolution fusion | flops 2155872256 | bytes 21267456 | tf_op jit(solution)/shard_map/dot_general | solution.py:90
  280.4 370.4 %reduce-scatter.2.cloned.1.call-done = f32[256,512]{1,0:T(8,128)} async-done(((f32[8192,512]{1,0:T(8,128)}), f32[256,512]{1,0:T(8,128)}) %reduce-scatter.2.cloned.1.call-update) | async-done | bytes 524304 | tf_op jit(solution)/shard_map/reduce_scatter | solution.py:89
  650.8 1.1 subtract_convert_fusion
  651.9 17.1 %all_to_all.19 = bf16[8,32,512]{2,1,0:T(8,128)(2,1)S(1)} all-to-all(bf16[8,32,512]{2,1,0:T(8,128)(2,1)S(1)} %bitcast.39), channel_id=1, replica_groups=mesh['grp'=2,'fsdp'=16,'tp'=8] {'tp'}, dimensions={0} | all-to-all | bytes 524288 | tf_op jit(solution)/shard_map/all_to_all | solution.py:98
  669.0 0.7 copy.31
  (30 shorter events, 0.4 us)
Async XLA Ops:
  7.2 44.0 %copy-start = (bf16[64,512]{1,0:T(8,128)(2,1)S(1)}, bf16[64,512]{1,0:T(8,128)(2,1)}, u32[]{:S(2)}) copy-start(bf16[64,512]{1,0:T(8,128)(2,1)} %param.18) | copy-start | bytes 196612
  7.2 43.8 %copy-start.7 = (s32[256,1]{0,1:T(1,128)S(1)}, s32[256,1]{0,1:T(1,128)}, u32[]{:S(2)}) copy-start(s32[256,1]{0,1:T(1,128)} %param.14) | copy-start | bytes 3076
  7.2 43.9 %copy-start.5 = (f32[64]{0:T(128)S(1)}, f32[64]{0:T(128)}, u32[]{:S(2)}) copy-start(f32[64]{0:T(128)} %param.15) | copy-start | bytes 772
  7.2 44.2 %copy-start.4 = (bf16[18,512]{1,0:T(8,128)(2,1)S(1)}, bf16[18,512]{1,0:T(8,128)(2,1)}, u32[]{:S(2)}) copy-start(bf16[18,512]{1,0:T(8,128)(2,1)} %param.19) | copy-start | bytes 55300
  7.2 44.2 %copy-start.6 = (s32[1,256]{1,0:T(1,128)S(1)}, s32[1,256]{1,0:T(1,128)}, u32[]{:S(2)}) copy-start(s32[1,256]{1,0:T(1,128)} %param.12) | copy-start | bytes 3076
  7.2 44.5 %copy-start.2 = (s32[1,256,32]{1,2,0:T(8,128)S(1)}, s32[1,256,32]{1,2,0:T(8,128)}, u32[]{:S(2)}) copy-start(s32[1,256,32]{1,2,0:T(8,128)} %param.13) | copy-start | bytes 98308
  7.2 76.2 %all-gather.2.cloned.1.call-start = ((), (), s32[]{:S(2)}) async-start(), calls=%async_computation.2 | async-start | bytes 8650752 | tf_op jit(solution)/shard_map/all_gather | solution.py:41
  8.0 259.2 %all-reduce.2.cloned.1.call-start = ((), (), s32[]{:S(2)}) async-start(), calls=%async_computation.3 | async-start | bytes 131072 | tf_op jit(solution)/shard_map/psum | solution.py:69
  47.8 35.6 %copy-start.3 = (f32[8192]{0:T(1024)S(1)}, f32[8192]{0:T(1024)}, u32[]{:S(2)}) copy-start(f32[8192]{0:T(1024)} %param.16) | copy-start | bytes 98308
  55.5 36.4 %copy-start.8 = (bf16[256]{0:T(256)(128)(2,1)S(1)}, bf16[256]{0:T(256)(128)(2,1)}, u32[]{:S(2)}) copy-start(bf16[256]{0:T(256)(128)(2,1)} %param.11) | copy-start | bytes 1540
  91.9 558.9 %reduce-scatter.2.cloned.1.call-start = ((), (), s32[]{:S(2)}) async-start(), calls=%async_computation.4 | async-start | bytes 17301504 | tf_op jit(solution)/shard_map/reduce_scatter | solution.py:89
  280.4 370.4 %copy-start.1 = (bf16[256,512]{1,0:T(8,128)(2,1)S(1)}, bf16[256,512]{1,0:T(8,128)(2,1)}, u32[]{:S(2)}) copy-start(bf16[256,512]{1,0:T(8,128)(2,1)} %param.17) | copy-start | bytes 786436
Sparse Core Ops, SparseCore 0:
  9.9 73.4 all-gather.1
  92.0 175.1 all-reduce.1
  280.5 370.1 reduce-scatter.1
where the time goes:
time: 677 us; the launch traced here: 676 us
  waiting for transfers between devices  571 us (84%)
  blocking collectives  56.1 us (8%)
  matrix products  22.7 us (3%)
  between operations  13.9 us (2%)
  other arithmetic  7.65 us (1%)
    reduce_scatter x1, waiting for transfers between devices, shards(): lax.psum_scatter(lax.dot_general(columns, grad_preact, (((0,), (0,)), (()...  370 us
    psum x1, waiting for transfers between devices, shards(): summed = lax.psum(stacked, ('grp', 'tp'))  172 us
    psum x1, blocking collectives, shards(): counts = lax.psum(jnp.sum(onehot.astype(jnp.float32), axis=0), 'fsdp')  39 us
    all_gather x1, waiting for transfers between devices, shards(): lax.all_gather(torso_weight, ('grp', 'fsdp'), axis=0, tiled=True)  27.9 us
    all_to_all x1, blocking collectives, shards(): lax.all_to_all(updated, 'tp', split_axis=0, concat_axis=1, tiled=True)  17.1 us
  transfers between devices with their start and end apart: 3, of which 3 were waited for; matrix products, arithmetic and copies ran while one was open for 2% of the time, Pallas kernels for 0%

commit v1 on v0

--- a/solution.py
+++ b/solution.py
@@ -6,6 +6,11 @@
 ACTIONS = 18
 COSINES = 64
 FRACS = 64
+
+
+def axis_by_axis(x, first, second):
+    inner = lax.psum(x, first)
+    return lax.psum(inner, second)
 
 
 def shards(
@@ -66,7 +71,7 @@
     stacked = jnp.where(
         own_slot, partial_quant[None, :, :], jnp.zeros_like(partial_quant)[None, :, :]
     )
-    summed = lax.psum(stacked, ("grp", "tp"))
+    summed = axis_by_axis(stacked, "tp", "grp")
     target_quant = summed[0]
     online_quant = summed[1]
     learner = (group_index == 1).astype(jnp.float32)

time: 677 us -> 632 us (0.934)
  waiting for transfers between devices: 571 us -> 527 us
    psum x1 -> x2, waiting for transfers between devices: 172 us -> 127 us  [the longest x1 98.3 us: axis_by_axis(): inner = lax.psum(x, first)]
  transfers between devices with their start and end apart: 3 -> 4, of which waited for: 3 -> 4; matrix products, arithmetic and copies ran while one was open for 2% -> 2% of each run, Pallas kernels for 0% -> 0%
where the time goes in v1:
time: 632 us
  waiting for transfers between devices  527 us (83%)
  blocking collectives  55.9 us (9%)
  matrix products  22.7 us (4%)
  between operations  13.9 us (2%)
  other arithmetic  7.65 us (1%)
    reduce_scatter x1, waiting for transfers between devices, shards(): lax.psum_scatter(lax.dot_general(columns, grad_preact, (((0,), (0,)), (()...  371 us
    psum x1, waiting for transfers between devices, axis_by_axis(): inner = lax.psum(x, first)  98.3 us
    psum x1, blocking collectives, shards(): counts = lax.psum(jnp.sum(onehot.astype(jnp.float32), axis=0), 'fsdp')  39 us
    psum x1, waiting for transfers between devices, axis_by_axis(): return lax.psum(inner, second)  29.2 us
    all_gather x1, waiting for transfers between devices, shards(): lax.all_gather(torso_weight, ('grp', 'fsdp'), axis=0, tiled=True)  27.9 us
    all_to_all x1, blocking collectives, shards(): lax.all_to_all(updated, 'tp', split_axis=0, concat_axis=1, tiled=True)  16.8 us
  transfers between devices with their start and end apart: 4, of which 4 were waited for; matrix products, arithmetic and copies ran while one was open for 2% of the time, Pallas kernels for 0%

profile of v1, /device:TPU:1, one launch (start us, length us, event | category | flops | bytes accessed | tf_op | source)
XLA Modules:
  0.0 631.9 jit_solution(6170733771334951054)
XLA Ops:
  7.3 0.7 all-gather.2.cloned.1.call-update
  8.0 0.8 convert_reduce_fusion
  8.8 39.0 %psum.21 = f32[16]{0:T(128)S(1)} all-reduce(f32[16]{0:T(128)S(1)} %convert_reduce_fusion), channel_id=1, replica_groups=mesh['grp'=2,'fsdp'=16,'tp'=8] {'fsdp'}, use_global_device_ids=true, to_apply=%region_2.0 | all-reduce | flops 16 | bytes 128 | tf_op jit(solution)/shard_map/psum | solution.py:33
  47.9 3.2 fusion
  51.0 0.3 fusion.12
  51.7 3.8 fusion.15
  55.4 27.9 %all-gather.2.cloned.1.call-done = bf16[8192,512]{1,0:T(8,128)(2,1)} async-done(((bf16[256,512]{1,0:T(8,128)(2,1)}), bf16[8192,512]{1,0:T(8,128)(2,1)}) %all-gather.2.cloned.1.call-update) | async-done | bytes 8388624 | tf_op jit(solution)/shard_map/all_gather | solution.py:46
  83.4 7.0 %fusion.10 = f32[256,512]{1,0:T(8,128)S(1)} fusion(bf16[8192,512]{1,0:T(8,128)(2,1)} %all-gather.2.cloned.1.call-done, bf16[1,256,8192]{2,1,0:T(8,128)(2,1)} %param.10, f32[8192]{0:T(1024)S(1)} %copy-done.3, f32[256]{0:T(256)S(1)} %add_rsqrt_fusion), kind=kOutput, calls=%fused_computation.17 | convolution fusion | flops 2155872256 | bytes 13140992 | tf_op jit(solution)/shard_map/dot_general | solution.py:44
  90.4 0.3 fusion.18
  90.7 0.4 select_reduce_fusion.1
  91.1 0.7 broadcast_select_fusion
  92.0 98.3 %all-reduce.3.cloned.1.call-done = f32[2,256,32]{1,2,0:T(8,128)} async-done(((f32[2,256,32]{1,2,0:T(8,128)}), f32[2,256,32]{1,2,0:T(8,128)}) %all-reduce.3.cloned.1.call-update) | async-done | bytes 65552 | tf_op jit(solution)/shard_map/psum | solution.py:12
  190.4 2.8 copy.17
  193.3 29.2 %all-reduce.5.cloned.1.call-done = f32[2,256,32]{1,2,0:T(8,128)} async-done(((f32[2,256,32]{1,2,0:T(8,128)}), f32[2,256,32]{1,2,0:T(8,128)}) %all-reduce.5.cloned.1.call-update) | async-done | bytes 65552 | tf_op jit(solution)/shard_map/psum | solution.py:13
  222.4 0.8 slice_bitcast_fusion
  223.2 0.8 fusion.22
  223.9 0.3 fusion.14
  224.3 0.4 select_reduce_fusion
  224.7 0.5 fusion.7
  225.2 10.4 %fusion.8 = f32[8192,512]{1,0:T(8,128)} fusion(bf16[256,512]{1,0:T(8,128)(2,1)S(1)} %fusion.7, bf16[1,256,8192]{2,1,0:T(8,128)(2,1)} %param.10, f32[8192]{0:T(1024)S(1)} %copy-done.3, f32[256]{0:T(256)S(1)} %add_rsqrt_fusion), kind=kOutput, calls=%fused_computation.16 | convolution fusion | flops 2155872256 | bytes 21267456 | tf_op jit(solution)/shard_map/dot_general | solution.py:95
  235.7 371.0 %reduce-scatter.2.cloned.1.call-done = f32[256,512]{1,0:T(8,128)} async-done(((f32[8192,512]{1,0:T(8,128)}), f32[256,512]{1,0:T(8,128)}) %reduce-scatter.2.cloned.1.call-update) | async-done | bytes 524304 | tf_op jit(solution)/shard_map/reduce_scatter | solution.py:94
  606.7 1.1 subtract_convert_fusion
  607.8 16.8 %all_to_all.19 = bf16[8,32,512]{2,1,0:T(8,128)(2,1)S(1)} all-to-all(bf16[8,32,512]{2,1,0:T(8,128)(2,1)S(1)} %bitcast.39), channel_id=1, replica_groups=mesh['grp'=2,'fsdp'=16,'tp'=8] {'tp'}, dimensions={0} | all-to-all | bytes 524288 | tf_op jit(solution)/shard_map/all_to_all | solution.py:103
  624.6 0.7 copy.31
  (33 shorter events, 0.7 us)
Async XLA Ops:
  7.2 43.9 %copy-start = (bf16[64,512]{1,0:T(8,128)(2,1)S(1)}, bf16[64,512]{1,0:T(8,128)(2,1)}, u32[]{:S(2)}) copy-start(bf16[64,512]{1,0:T(8,128)(2,1)} %param.18) | copy-start | bytes 196612
  7.2 43.9 %copy-start.5 = (f32[64]{0:T(128)S(1)}, f32[64]{0:T(128)}, u32[]{:S(2)}) copy-start(f32[64]{0:T(128)} %param.15) | copy-start | bytes 772
  7.2 44.2 %copy-start.4 = (bf16[18,512]{1,0:T(8,128)(2,1)S(1)}, bf16[18,512]{1,0:T(8,128)(2,1)}, u32[]{:S(2)}) copy-start(bf16[18,512]{1,0:T(8,128)(2,1)} %param.19) | copy-start | bytes 55300
  7.2 44.2 %copy-start.6 = (s32[1,256]{1,0:T(1,128)S(1)}, s32[1,256]{1,0:T(1,128)}, u32[]{:S(2)}) copy-start(s32[1,256]{1,0:T(1,128)} %param.12) | copy-start | bytes 3076
  7.2 44.4 %copy-start.2 = (s32[1,256,32]{1,2,0:T(8,128)S(1)}, s32[1,256,32]{1,2,0:T(8,128)}, u32[]{:S(2)}) copy-start(s32[1,256,32]{1,2,0:T(8,128)} %param.13) | copy-start | bytes 98308
  7.2 76.2 %all-gather.2.cloned.1.call-start = ((), (), s32[]{:S(2)}) async-start(), calls=%async_computation.2 | async-start | bytes 8650752 | tf_op jit(solution)/shard_map/all_gather | solution.py:46
  8.0 182.4 %all-reduce.3.cloned.1.call-start = ((), (), s32[]{:S(2)}) async-start(), calls=%async_computation.3 | async-start | bytes 131072 | tf_op jit(solution)/shard_map/psum | solution.py:12
  47.9 35.5 %copy-start.3 = (f32[8192]{0:T(1024)S(1)}, f32[8192]{0:T(1024)}, u32[]{:S(2)}) copy-start(f32[8192]{0:T(1024)} %param.16) | copy-start | bytes 98308
  55.4 36.4 %copy-start.7 = (s32[256,1]{0,1:T(1,128)S(1)}, s32[256,1]{0,1:T(1,128)}, u32[]{:S(2)}) copy-start(s32[256,1]{0,1:T(1,128)} %param.14) | copy-start | bytes 3076
  55.4 135.0 %copy-start.8 = (bf16[256]{0:T(256)(128)(2,1)S(1)}, bf16[256]{0:T(256)(128)(2,1)}, u32[]{:S(2)}) copy-start(bf16[256]{0:T(256)(128)(2,1)} %param.11) | copy-start | bytes 1540
  91.8 130.6 %all-reduce.5.cloned.1.call-start = ((), (), s32[]{:S(2)}) async-start(), calls=%async_computation.4 | async-start | bytes 131072 | tf_op jit(solution)/shard_map/psum | solution.py:13
  190.3 416.3 %reduce-scatter.2.cloned.1.call-start = ((), (), s32[]{:S(2)}) async-start(), calls=%async_computation.5 | async-start | bytes 17301504 | tf_op jit(solution)/shard_map/reduce_scatter | solution.py:94
  235.6 371.0 %copy-start.1 = (bf16[256,512]{1,0:T(8,128)(2,1)S(1)}, bf16[256,512]{1,0:T(8,128)(2,1)}, u32[]{:S(2)}) copy-start(bf16[256,512]{1,0:T(8,128)(2,1)} %param.17) | copy-start | bytes 786436
Sparse Core Ops, SparseCore 0:
  9.9 73.4 all-gather.1
  91.9 98.3 all-reduce.2
  193.0 29.3 all-reduce.4
  235.8 370.8 reduce-scatter.1
